TPU v7x, 32 devices: a whole 2x2x4 slice. The times are simulated.
32 devices in a mesh: bin: 4 (over x, core), slab: 8 (over z, y).
Axes of the slice: x: 2, y: 2, z: 4, core: 2. Of those that a mesh axis runs over, the one named last changes fastest.
Arguments:
- volumes: float32 [8, 32, 64, 512], P('bin', 'slab'), may hold values from -6 to 6
- attenuation: float32 [8, 3], replicated, may hold values from 0.2 to 1.2
- penalty: float32 [1], replicated, may hold values from 0.2 to 0.4
- tv_weight: float32 [1], replicated, may hold values from 0.3 to 0.8
Outputs:
- materials: float32 [3, 32, 64, 512], P(None, ('bin', 'slab'))
All inputs are finite; a program needn't handle non-finite values.
Results may differ from a plain program's by a relative error of at most 0.0001.
Values sent between devices are 32-bit elements; how exact they have to be, the bound alone decides.
No kernel may reach another device: no remote copies, remote signals or barrier semaphores. Data moves between devices by JAX's collectives and lax.ppermute only.
A program may use at most 64 MiB of HBM per device.

v0:
```python
import jax
import jax.numpy as jnp
from jax import lax
from jax.sharding import PartitionSpec as P

ITERS = 3


def from_behind(x, axis, by):
    peers = lax.axis_size(axis)
    pairs = [(i, i + by) for i in range(peers) if 0 <= i + by < peers]
    return lax.ppermute(x, axis, pairs)


def inverse_three(matrix):
    cofactor = [
        [
            matrix[(row + 1) % 3, (col + 1) % 3] * matrix[(row + 2) % 3, (col + 2) % 3]
            - matrix[(row + 1) % 3, (col + 2) % 3] * matrix[(row + 2) % 3, (col + 1) % 3]
            for col in range(3)
        ]
        for row in range(3)
    ]
    determinant = (
        matrix[0, 0] * cofactor[0][0]
        + matrix[0, 1] * cofactor[0][1]
        + matrix[0, 2] * cofactor[0][2]
    )
    return [[cofactor[col][row] / determinant for col in range(3)] for row in range(3)]


def normal_inverse(attenuation, penalty_value):
    gram = jnp.dot(attenuation.T, attenuation, precision=lax.Precision.HIGHEST)
    gram = gram + 12.0 * penalty_value * jnp.eye(3, dtype=jnp.float32)
    return inverse_three(gram)


def apply_inverse(inverse, fields):
    return jnp.stack(
        [
            inverse[row][0] * fields[0] + inverse[row][1] * fields[1] + inverse[row][2] * fields[2]
            for row in range(3)
        ]
    )


def project(attenuation, volumes):
    return jnp.einsum("km,kzyx->mzyx", attenuation, volumes, precision=lax.Precision.HIGHEST)


def gradient(field):
    interior_z = (lax.axis_index("bin") < lax.axis_size("bin") - 1).astype(jnp.float32)
    interior_y = (lax.axis_index("slab") < lax.axis_size("slab") - 1).astype(jnp.float32)
    below = from_behind(field[:, :1], "bin", -1)
    after = from_behind(field[:, :, :1], "slab", -1)
    along_z = jnp.concatenate(
        [field[:, 1:] - field[:, :-1], (below - field[:, -1:]) * interior_z], 1
    )
    along_y = jnp.concatenate(
        [field[:, :, 1:] - field[:, :, :-1], (after - field[:, :, -1:]) * interior_y], 2
    )
    along_x = jnp.concatenate(
        [field[:, :, :, 1:] - field[:, :, :, :-1], jnp.zeros_like(field[:, :, :, :1])], 3
    )
    return [along_z, along_y, along_x]


def divergence(parts):
    above = from_behind(parts[0][:, -1:], "bin", 1)
    before = from_behind(parts[1][:, :, -1:], "slab", 1)
    total = parts[0] - jnp.concatenate([above, parts[0][:, :-1]], 1)
    total = total + (parts[1] - jnp.concatenate([before, parts[1][:, :, :-1]], 2))
    total = total + (
        parts[2]
        - jnp.concatenate([jnp.zeros_like(parts[2][:, :, :, :1]), parts[2][:, :, :, :-1]], 3)
    )
    return total


def clip_group(parts, threshold):
    squares = (
        jnp.sum(parts[0] * parts[0], axis=0)
        + jnp.sum(parts[1] * parts[1], axis=0)
        + jnp.sum(parts[2] * parts[2], axis=0)
    )
    scale = threshold / jnp.maximum(jnp.sqrt(squares), threshold)
    return [part * scale[None] for part in parts]


def on_device(volumes, attenuation, penalty, tv_weight):
    penalty_value = penalty[0]
    threshold = tv_weight[0] / penalty_value
    inverse = normal_inverse(attenuation, penalty_value)
    cube = lax.all_to_all(
        lax.all_to_all(volumes, "slab", split_axis=2, concat_axis=1, tiled=True),
        "bin",
        split_axis=1,
        concat_axis=0,
        tiled=True,
    )
    data = project(attenuation, cube)
    field = apply_inverse(inverse, data)
    dual = clip_group(gradient(field), threshold)
    step_parts = [2.0 * part for part in dual]
    for turn in range(ITERS):
        field = apply_inverse(
            inverse, data + 12.0 * penalty_value * field + penalty_value * divergence(step_parts)
        )
        if turn < ITERS - 1:
            grads = gradient(field)
            fresh = clip_group([grads[index] + dual[index] for index in range(3)], threshold)
            step_parts = [2.0 * fresh[index] - dual[index] for index in range(3)]
            dual = fresh
    return lax.all_to_all(field, "slab", split_axis=1, concat_axis=2, tiled=True)


def solution(mesh):
    placed = (P("bin", "slab", None, None), P(), P(), P())
    return jax.shard_map(
        on_device,
        mesh=mesh,
        in_specs=placed,
        out_specs=P(None, ("bin", "slab"), None, None),
        check_vma=False,
    )
```

profile of v0, /device:TPU:0, one launch (start us, length us, event | category | flops | bytes accessed | tf_op | source)
XLA Modules:
  0.0 149.0 jit_solution(16900868698549911127)
XLA Ops:
  0.0 1.9 %copy.18 = f32[2,4,64,512]{3,1,0,2:T(4,128)S(1)} copy(f32[2,4,64,512]{3,2,1,0:T(8,128)} %param.4) | data formatting | bytes 2097152 | tf_op args[0]
  1.9 32.9 %all_to_all.48 = f32[2,4,64,512]{3,1,0,2:T(4,128)S(1)} all-to-all(f32[2,4,64,512]{3,1,0,2:T(4,128)S(1)} %copy.18), channel_id=1, replica_groups=mesh['bin'=4,'slab'=8] {'slab'}, dimensions={2} | all-to-all | bytes 2097152 | tf_op jit(solution)/shard_map/all_to_all | solution.py:95
  34.8 0.6 copy.31
  35.4 0.1 copy.20
  35.5 1.1 copy.21
  36.6 3.5 %all-to-all-start.1 = ((f32[2,32,8,512]{3,2,0,1:T(8,128)}), f32[2,32,8,512]{3,2,0,1:T(8,128)S(1)}, u32[]{:S(2)}, u32[]{:S(2)}) async-start(f32[2,32,8,512]{3,2,0,1:T(8,128)} %copy.21), calls=%async_computation.1 | async-start | bytes 2097152 | tf_op jit(solution)/shard_map/all_to_all | solution.py:94
  40.8 0.1 convolution_add_fusion
  40.9 0.7 fusion.21
  67.1 0.8 copy.23
  67.9 0.7 all_to_all.42
  68.7 1.0 fusion.19
  69.7 0.6 multiply_add_fusion.11
  70.3 0.4 pad_maximum_fusion
  70.7 0.1 slice_subtract_fusion.7
  70.8 0.3 slice_subtract_fusion.2
  71.2 1.3 collective-permute-start.1
  72.5 0.1 slice_subtract_fusion.8
  72.6 1.3 collective-permute-start
  73.9 0.4 multiply_reduce_fusion.6
  74.2 3.3 %collective-permute-done.1 = f32[3,8,1,512]{3,0,2,1:T(4,128)S(1)} collective-permute-done((f32[3,8,1,512]{3,0,2,1:T(4,128)S(1)}, f32[3,8,1,512]{3,0,2,1:T(4,128)S(1)}, u32[]{:S(2)}, u32[]{:S(2)}) %collective-permute-start.1) | collective-permute-done | bytes 49184 | tf_op jit(solution)/shard_map/ppermute | solution.py:12
  77.5 0.4 multiply_reduce_fusion.7
  78.0 0.4 multiply_reduce_fusion.8
  78.4 0.5 fusion.12
  78.9 2.6 %collective-permute-start.2 = (f32[3,1,8,512]{3,0,2,1:T(4,128)S(1)}, f32[3,1,8,512]{3,0,2,1:T(4,128)S(1)}, u32[]{:S(2)}, u32[]{:S(2)}) collective-permute-start(f32[3,1,8,512]{3,0,2,1:T(4,128)S(1)} %slice.331), channel_id=1, source_target_pairs={{0,8},{8,16},{16,24},{1,9},{9,17},{17,25},{2,10},{10,18},{18,26},{... | collective-permute-start | bytes 147464 | tf_op jit(solution)/shard_map/ppermute | solution.py:12
  81.5 4.4 %collective-permute-start.3 = (f32[3,8,1,512]{3,0,2,1:T(4,128)S(1)}, f32[3,8,1,512]{3,0,2,1:T(4,128)S(1)}, u32[]{:S(2)}, u32[]{:S(2)}) collective-permute-start(f32[3,8,1,512]{3,0,2,1:T(4,128)S(1)} %slice.333), channel_id=1, source_target_pairs={{0,1},{1,2},{2,3},{3,4},{4,5},{5,6},{6,7},{8,9},{9,10},{10,11},{11... | collective-permute-start | bytes 147464 | tf_op jit(solution)/shard_map/ppermute | solution.py:12
  86.1 0.1 slice.332
  86.2 2.3 %collective-permute-done.3 = f32[3,8,1,512]{3,0,2,1:T(4,128)S(1)} collective-permute-done((f32[3,8,1,512]{3,0,2,1:T(4,128)S(1)}, f32[3,8,1,512]{3,0,2,1:T(4,128)S(1)}, u32[]{:S(2)}, u32[]{:S(2)}) %collective-permute-start.3) | collective-permute-done | bytes 49184 | tf_op jit(solution)/shard_map/ppermute | solution.py:12
  88.4 0.9 fusion.3
  89.3 0.6 multiply_add_fusion.8
  90.0 0.4 pad_maximum_fusion.3
  90.4 0.1 slice_subtract_fusion.5
  90.5 0.3 slice_subtract_fusion.1
  90.8 1.3 collective-permute-start.5
  92.1 0.1 slice_subtract_fusion.6
  92.2 1.5 collective-permute-start.4
  93.7 3.9 %collective-permute-done.5 = f32[3,8,1,512]{3,0,2,1:T(4,128)S(1)} collective-permute-done((f32[3,8,1,512]{3,0,2,1:T(4,128)S(1)}, f32[3,8,1,512]{3,0,2,1:T(4,128)S(1)}, u32[]{:S(2)}, u32[]{:S(2)}) %collective-permute-start.5) | collective-permute-done | bytes 49184 | tf_op jit(solution)/shard_map/ppermute | solution.py:12
  97.6 1.7 %multiply_reduce_fusion.3 = (f32[8,8,512]{2,1,0:T(8,128)S(1)}, f32[3,8,8,512]{3,0,2,1:T(4,128)S(1)}, f32[8,8,512]{2,1,0:T(8,128)S(1)}, f32[3,8,8,512]{3,0,2,1:T(...) fusion(f32[8,8,512]{2,1,0:T(8,128)S(1)} %maximum_divide_fusion.2, ...), kind=kLoop, calls=%fused_computation.43 | loop fusion | flops 1474560 | bytes 4061696 | tf_op jit(solution)/shard_map/reduce_sum | solution.py:84
  99.4 0.7 multiply_subtract_fusion.3
  100.2 2.3 %collective-permute-start.6 = (f32[3,1,8,512]{3,0,2,1:T(4,128)S(1)}, f32[3,1,8,512]{3,0,2,1:T(4,128)S(1)}, u32[]{:S(2)}, u32[]{:S(2)}) collective-permute-start(f32[3,1,8,512]{3,0,2,1:T(4,128)S(1)} %slice.349), channel_id=1, source_target_pairs={{0,8},{8,16},{16,24},{1,9},{9,17},{17,25},{2,10},{10,18},{18,26},{... | collective-permute-start | bytes 147464 | tf_op jit(solution)/shard_map/ppermute | solution.py:12
  102.4 5.0 %collective-permute-start.7 = (f32[3,8,1,512]{3,0,2,1:T(4,128)S(1)}, f32[3,8,1,512]{3,0,2,1:T(4,128)S(1)}, u32[]{:S(2)}, u32[]{:S(2)}) collective-permute-start(f32[3,8,1,512]{3,0,2,1:T(4,128)S(1)} %slice.351), channel_id=1, source_target_pairs={{0,1},{1,2},{2,3},{3,4},{4,5},{5,6},{6,7},{8,9},{9,10},{10,11},{11... | collective-permute-start | bytes 147464 | tf_op jit(solution)/shard_map/ppermute | solution.py:12
  107.4 0.1 slice.352
  107.5 0.1 slice.350
  107.6 1.7 %collective-permute-done.7 = f32[3,8,1,512]{3,0,2,1:T(4,128)S(1)} collective-permute-done((f32[3,8,1,512]{3,0,2,1:T(4,128)S(1)}, f32[3,8,1,512]{3,0,2,1:T(4,128)S(1)}, u32[]{:S(2)}, u32[]{:S(2)}) %collective-permute-start.7) | collective-permute-done | bytes 49184 | tf_op jit(solution)/shard_map/ppermute | solution.py:12
  109.3 0.8 fusion.7
  110.2 0.6 multiply_add_fusion.5
  110.8 0.4 pad_maximum_fusion.4
  111.2 0.1 slice_subtract_fusion.3
  111.3 0.3 slice_subtract_fusion
  111.6 1.3 collective-permute-start.9
  112.9 0.1 slice_subtract_fusion.4
  113.1 1.3 collective-permute-start.8
  114.4 4.1 %collective-permute-done.9 = f32[3,8,1,512]{3,0,2,1:T(4,128)S(1)} collective-permute-done((f32[3,8,1,512]{3,0,2,1:T(4,128)S(1)}, f32[3,8,1,512]{3,0,2,1:T(4,128)S(1)}, u32[]{:S(2)}, u32[]{:S(2)}) %collective-permute-start.9) | collective-permute-done | bytes 49184 | tf_op jit(solution)/shard_map/ppermute | solution.py:12
  118.5 1.4 multiply_reduce_fusion.1
  120.0 0.7 multiply_subtract_fusion
  120.7 1.5 %collective-permute-start.10 = (f32[3,1,8,512]{3,0,2,1:T(4,128)S(1)}, f32[3,1,8,512]{3,0,2,1:T(4,128)S(1)}, u32[]{:S(2)}, u32[]{:S(2)}) collective-permute-start(f32[3,1,8,512]{3,0,2,1:T(4,128)S(1)} %slice.367), channel_id=1, source_target_pairs={{0,8},{8,16},{16,24},{1,9},{9,17},{17,25},{2,10},{10,18},{18,26},{... | collective-permute-start | bytes 147464 | tf_op jit(solution)/shard_map/ppermute | solution.py:12
  122.3 5.2 %collective-permute-start.11 = (f32[3,8,1,512]{3,0,2,1:T(4,128)S(1)}, f32[3,8,1,512]{3,0,2,1:T(4,128)S(1)}, u32[]{:S(2)}, u32[]{:S(2)}) collective-permute-start(f32[3,8,1,512]{3,0,2,1:T(4,128)S(1)} %slice.369), channel_id=1, source_target_pairs={{0,1},{1,2},{2,3},{3,4},{4,5},{5,6},{6,7},{8,9},{9,10},{10,11},{11... | collective-permute-start | bytes 147464 | tf_op jit(solution)/shard_map/ppermute | solution.py:12
  127.4 0.1 slice.370
  127.6 1.7 %collective-permute-done.11 = f32[3,8,1,512]{3,0,2,1:T(4,128)S(1)} collective-permute-done((f32[3,8,1,512]{3,0,2,1:T(4,128)S(1)}, f32[3,8,1,512]{3,0,2,1:T(4,128)S(1)}, u32[]{:S(2)}, u32[]{:S(2)}) %collective-permute-start.11) | collective-permute-done | bytes 49184 | tf_op jit(solution)/shard_map/ppermute | solution.py:12
  129.3 0.9 fusion.11
  130.2 0.6 multiply_add_fusion.2
  130.8 0.4 pad_maximum_fusion.5
  131.2 0.1 copy.24
  131.3 16.9 %all_to_all.49 = f32[3,8,8,512]{3,2,0,1:T(8,128)S(1)} all-to-all(f32[3,8,8,512]{3,2,0,1:T(8,128)S(1)} %copy.24), channel_id=1, replica_groups=mesh['bin'=4,'slab'=8] {'slab'}, dimensions={1} | all-to-all | bytes 786432 | tf_op jit(solution)/shard_map/all_to_all | solution.py:114
  148.2 0.8 copy.32
  (32 shorter events, 0.7 us)
Async XLA Ops:
  0.0 40.8 %copy-start = (f32[8,3]{0,1:T(4,128)S(1)}, f32[8,3]{0,1:T(4,128)}, u32[]{:S(2)}) copy-start(f32[8,3]{0,1:T(4,128)} %param.5) | copy-start | bytes 292
  36.6 30.5 %all-to-all-start.1 = ((f32[2,32,8,512]{3,2,0,1:T(8,128)}), f32[2,32,8,512]{3,2,0,1:T(8,128)S(1)}, u32[]{:S(2)}, u32[]{:S(2)}) async-start(f32[2,32,8,512]{3,2,0,1:T(8,128)} %copy.21), calls=%async_computation.1 | async-start | bytes 2097152 | tf_op jit(solution)/shard_map/all_to_all | solution.py:94
  71.2 6.4 %collective-permute-start.1 = (f32[3,8,1,512]{3,0,2,1:T(4,128)S(1)}, f32[3,8,1,512]{3,0,2,1:T(4,128)S(1)}, u32[]{:S(2)}, u32[]{:S(2)}) collective-permute-start(f32[3,8,1,512]{3,0,2,1:T(4,128)S(1)} %slice.327), channel_id=1, source_target_pairs={{1,0},{2,1},{3,2},{4,3},{5,4},{6,5},{7,6},{9,8},{10,9},{11,10},{12... | collective-permute-start | bytes 147464 | tf_op jit(solution)/shard_map/ppermute | solution.py:12
  72.6 5.3 %collective-permute-start = (f32[3,1,8,512]{3,0,2,1:T(4,128)S(1)}, f32[3,1,8,512]{3,0,2,1:T(4,128)S(1)}, u32[]{:S(2)}, u32[]{:S(2)}) collective-permute-start(f32[3,1,8,512]{3,0,2,1:T(4,128)S(1)} %slice.323), channel_id=1, source_target_pairs={{8,0},{16,8},{24,16},{9,1},{17,9},{25,17},{10,2},{18,10},{26,18},{... | collective-permute-start | bytes 147464 | tf_op jit(solution)/shard_map/ppermute | solution.py:12
  78.9 7.2 %collective-permute-start.2 = (f32[3,1,8,512]{3,0,2,1:T(4,128)S(1)}, f32[3,1,8,512]{3,0,2,1:T(4,128)S(1)}, u32[]{:S(2)}, u32[]{:S(2)}) collective-permute-start(f32[3,1,8,512]{3,0,2,1:T(4,128)S(1)} %slice.331), channel_id=1, source_target_pairs={{0,8},{8,16},{16,24},{1,9},{9,17},{17,25},{2,10},{10,18},{18,26},{... | collective-permute-start | bytes 147464 | tf_op jit(solution)/shard_map/ppermute | solution.py:12
  81.5 6.9 %collective-permute-start.3 = (f32[3,8,1,512]{3,0,2,1:T(4,128)S(1)}, f32[3,8,1,512]{3,0,2,1:T(4,128)S(1)}, u32[]{:S(2)}, u32[]{:S(2)}) collective-permute-start(f32[3,8,1,512]{3,0,2,1:T(4,128)S(1)} %slice.333), channel_id=1, source_target_pairs={{0,1},{1,2},{2,3},{3,4},{4,5},{5,6},{6,7},{8,9},{9,10},{10,11},{11... | collective-permute-start | bytes 147464 | tf_op jit(solution)/shard_map/ppermute | solution.py:12
  90.8 6.8 %collective-permute-start.5 = (f32[3,8,1,512]{3,0,2,1:T(4,128)S(1)}, f32[3,8,1,512]{3,0,2,1:T(4,128)S(1)}, u32[]{:S(2)}, u32[]{:S(2)}) collective-permute-start(f32[3,8,1,512]{3,0,2,1:T(4,128)S(1)} %slice.345), channel_id=1, source_target_pairs={{1,0},{2,1},{3,2},{4,3},{5,4},{6,5},{7,6},{9,8},{10,9},{11,10},{12... | collective-permute-start | bytes 147464 | tf_op jit(solution)/shard_map/ppermute | solution.py:12
  92.2 5.4 %collective-permute-start.4 = (f32[3,1,8,512]{3,0,2,1:T(4,128)S(1)}, f32[3,1,8,512]{3,0,2,1:T(4,128)S(1)}, u32[]{:S(2)}, u32[]{:S(2)}) collective-permute-start(f32[3,1,8,512]{3,0,2,1:T(4,128)S(1)} %slice.341), channel_id=1, source_target_pairs={{8,0},{16,8},{24,16},{9,1},{17,9},{25,17},{10,2},{18,10},{26,18},{... | collective-permute-start | bytes 147464 | tf_op jit(solution)/shard_map/ppermute | solution.py:12
  100.2 7.5 %collective-permute-start.6 = (f32[3,1,8,512]{3,0,2,1:T(4,128)S(1)}, f32[3,1,8,512]{3,0,2,1:T(4,128)S(1)}, u32[]{:S(2)}, u32[]{:S(2)}) collective-permute-start(f32[3,1,8,512]{3,0,2,1:T(4,128)S(1)} %slice.349), channel_id=1, source_target_pairs={{0,8},{8,16},{16,24},{1,9},{9,17},{17,25},{2,10},{10,18},{18,26},{... | collective-permute-start | bytes 147464 | tf_op jit(solution)/shard_map/ppermute | solution.py:12
  102.4 6.9 %collective-permute-start.7 = (f32[3,8,1,512]{3,0,2,1:T(4,128)S(1)}, f32[3,8,1,512]{3,0,2,1:T(4,128)S(1)}, u32[]{:S(2)}, u32[]{:S(2)}) collective-permute-start(f32[3,8,1,512]{3,0,2,1:T(4,128)S(1)} %slice.351), channel_id=1, source_target_pairs={{0,1},{1,2},{2,3},{3,4},{4,5},{5,6},{6,7},{8,9},{9,10},{10,11},{11... | collective-permute-start | bytes 147464 | tf_op jit(solution)/shard_map/ppermute | solution.py:12
  111.6 6.8 %collective-permute-start.9 = (f32[3,8,1,512]{3,0,2,1:T(4,128)S(1)}, f32[3,8,1,512]{3,0,2,1:T(4,128)S(1)}, u32[]{:S(2)}, u32[]{:S(2)}) collective-permute-start(f32[3,8,1,512]{3,0,2,1:T(4,128)S(1)} %slice.363), channel_id=1, source_target_pairs={{1,0},{2,1},{3,2},{4,3},{5,4},{6,5},{7,6},{9,8},{10,9},{11,10},{12... | collective-permute-start | bytes 147464 | tf_op jit(solution)/shard_map/ppermute | solution.py:12
  113.1 5.4 %collective-permute-start.8 = (f32[3,1,8,512]{3,0,2,1:T(4,128)S(1)}, f32[3,1,8,512]{3,0,2,1:T(4,128)S(1)}, u32[]{:S(2)}, u32[]{:S(2)}) collective-permute-start(f32[3,1,8,512]{3,0,2,1:T(4,128)S(1)} %slice.359), channel_id=1, source_target_pairs={{8,0},{16,8},{24,16},{9,1},{17,9},{25,17},{10,2},{18,10},{26,18},{... | collective-permute-start | bytes 147464 | tf_op jit(solution)/shard_map/ppermute | solution.py:12
  120.7 6.9 %collective-permute-start.10 = (f32[3,1,8,512]{3,0,2,1:T(4,128)S(1)}, f32[3,1,8,512]{3,0,2,1:T(4,128)S(1)}, u32[]{:S(2)}, u32[]{:S(2)}) collective-permute-start(f32[3,1,8,512]{3,0,2,1:T(4,128)S(1)} %slice.367), channel_id=1, source_target_pairs={{0,8},{8,16},{16,24},{1,9},{9,17},{17,25},{2,10},{10,18},{18,26},{... | collective-permute-start | bytes 147464 | tf_op jit(solution)/shard_map/ppermute | solution.py:12
  122.3 7.1 %collective-permute-start.11 = (f32[3,8,1,512]{3,0,2,1:T(4,128)S(1)}, f32[3,8,1,512]{3,0,2,1:T(4,128)S(1)}, u32[]{:S(2)}, u32[]{:S(2)}) collective-permute-start(f32[3,8,1,512]{3,0,2,1:T(4,128)S(1)} %slice.369), channel_id=1, source_target_pairs={{0,1},{1,2},{2,3},{3,4},{4,5},{5,6},{6,7},{8,9},{9,10},{10,11},{11... | collective-permute-start | bytes 147464 | tf_op jit(solution)/shard_map/ppermute | solution.py:12
where the time goes:
time: 150 us; the launch traced here: 149 us
  blocking collectives  49.8 us (33%)
  starting transfers between devices  32.5 us (22%)
  between operations  26.7 us (18%)
  waiting for transfers between devices  16.9 us (11%)
  other arithmetic  14.6 us (10%)
  local copies, waits for them, and re-layouts  7.48 us (5%)
    all_to_all x1, blocking collectives, on_device(): lax.all_to_all(volumes, 'slab', split_axis=2, concat_axis=1, tiled=True)  32.9 us
    ppermute x12, starting transfers between devices, from_behind(): return lax.ppermute(x, axis, pairs)  28.9 us
    all_to_all x1, blocking collectives, on_device(): lax.all_to_all(field, 'slab', split_axis=1, concat_axis=2, tiled=True)  16.9 us
    ppermute x12, waiting for transfers between devices, from_behind(): return lax.ppermute(x, axis, pairs)  16.9 us
    all_to_all x1, starting transfers between devices, on_device(): lax.all_to_all(lax.all_to_all(volumes, 'slab', split_axis=2, concat_axis=...  3.51 us
  transfers between devices with their start and end apart: 13, of which 6 were waited for; matrix products, arithmetic and copies ran while one was open for 2% of the time, Pallas kernels for 0%

commit v1 on v0

--- a/solution.py
+++ b/solution.py
@@ -92,7 +92,12 @@
     threshold = tv_weight[0] / penalty_value
     inverse = normal_inverse(attenuation, penalty_value)
     cube = lax.all_to_all(
-        lax.all_to_all(volumes, "slab", split_axis=2, concat_axis=1, tiled=True),
+        jnp.concatenate(
+            lax.all_to_all(
+                jnp.stack(jnp.split(volumes, lax.axis_size("slab"), axis=2)), "slab", 0, 0
+            ),
+            axis=1,
+        ),
         "bin",
         split_axis=1,
         concat_axis=0,

time: 150 us -> 155 us (1.033)
  local copies, waits for them, and re-layouts: 7.48 us -> 12.3 us
    unnamed x3 -> x9, local copies, waits for them, and re-layouts: 1.92 us -> 6.43 us
    all_to_all x5 -> x3, local copies, waits for them, and re-layouts: 3.31 us -> 1.62 us  [the longest x2 1.53 us: on_device(): lax.all_to_all(jnp.concatenate(lax.all_to_all(jnp.stack(jnp.split(volumes...]
where the time goes in v1:
time: 155 us; the launch traced here: 154 us
  blocking collectives  49.8 us (32%)
  starting transfers between devices  32.5 us (21%)
  between operations  26.8 us (17%)
  waiting for transfers between devices  16.9 us (11%)
  other arithmetic  14.6 us (9%)
  local copies, waits for them, and re-layouts  12.3 us (8%)
    all_to_all x1, blocking collectives, on_device(): lax.all_to_all(jnp.stack(jnp.split(volumes, lax.axis_size('slab'), axis=2...  32.9 us
    ppermute x12, starting transfers between devices, from_behind(): return lax.ppermute(x, axis, pairs)  28.9 us
    all_to_all x1, blocking collectives, on_device(): lax.all_to_all(field, 'slab', split_axis=1, concat_axis=2, tiled=True)  16.9 us
    ppermute x12, waiting for transfers between devices, from_behind(): return lax.ppermute(x, axis, pairs)  16.9 us
    unnamed x9, local copies, waits for them, and re-layouts  6.43 us
    all_to_all x1, starting transfers between devices, on_device(): lax.all_to_all(jnp.concatenate(lax.all_to_all(jnp.stack(jnp.split(volumes...  3.51 us
  transfers between devices with their start and end apart: 13, of which 6 were waited for; matrix products, arithmetic and copies ran while one was open for 2% of the time, Pallas kernels for 0%

profile of v1, /device:TPU:0, one launch (start us, length us, event | category | flops | bytes accessed | tf_op | source)
XLA Modules:
  0.0 153.8 jit_solution(4720220138608328086)
XLA Ops:
  0.0 0.9 bitcast_dynamic-update-slice_fusion.7
  0.9 0.9 bitcast_dynamic-update-slice_fusion.6
  1.9 0.9 bitcast_dynamic-update-slice_fusion.5
  2.8 0.9 bitcast_dynamic-update-slice_fusion.4
  3.7 0.9 bitcast_dynamic-update-slice_fusion.3
  4.6 0.9 bitcast_dynamic-update-slice_fusion.2
  5.5 0.9 bitcast_dynamic-update-slice_fusion.1
  6.5 0.9 bitcast_dynamic-update-slice_fusion
  7.4 32.9 %all_to_all.35 = f32[8,2,4,8,512]{4,3,2,1,0:T(8,128)S(1)} all-to-all(f32[8,2,4,8,512]{4,3,2,1,0:T(8,128)S(1)} %bitcast_dynamic-update-slice_fusion), channel_id=1, replica_groups=mesh['bin'=4,'slab'=8] {'slab'}, dimensions={0} | all-to-all | bytes 2097152 | tf_op jit(solution)/shard_map/all_to_all | solution.py:96
  40.3 1.1 copy.14
  41.4 3.5 %all-to-all-start.1 = ((f32[2,32,8,512]{3,2,0,1:T(8,128)}), f32[2,32,8,512]{3,2,0,1:T(8,128)S(1)}, u32[]{:S(2)}, u32[]{:S(2)}) async-start(f32[2,32,8,512]{3,2,0,1:T(8,128)} %copy.14), calls=%async_computation.1 | async-start | bytes 2097152 | tf_op jit(solution)/shard_map/all_to_all | solution.py:94
  45.6 0.1 convolution_add_fusion
  45.7 0.7 fusion.20
  72.0 0.8 copy.16
  72.8 0.7 all_to_all.29
  73.5 1.0 convolution_bitcast_fusion
  74.5 0.6 multiply_add_fusion.11
  75.2 0.4 pad_maximum_fusion
  75.5 0.1 slice_subtract_fusion.7
  75.6 0.3 slice_subtract_fusion.2
  76.0 1.3 collective-permute-start.1
  77.4 1.3 collective-permute-start
  78.7 0.4 multiply_reduce_fusion.6
  79.1 3.3 %collective-permute-done.1 = f32[3,8,1,512]{3,0,2,1:T(4,128)S(1)} collective-permute-done((f32[3,8,1,512]{3,0,2,1:T(4,128)S(1)}, f32[3,8,1,512]{3,0,2,1:T(4,128)S(1)}, u32[]{:S(2)}, u32[]{:S(2)}) %collective-permute-start.1) | collective-permute-done | bytes 49184 | tf_op jit(solution)/shard_map/ppermute | solution.py:12
  82.4 0.4 multiply_reduce_fusion.7
  82.8 0.4 multiply_reduce_fusion.8
  83.2 0.5 fusion.12
  83.8 2.6 %collective-permute-start.2 = (f32[3,1,8,512]{3,0,2,1:T(4,128)S(1)}, f32[3,1,8,512]{3,0,2,1:T(4,128)S(1)}, u32[]{:S(2)}, u32[]{:S(2)}) collective-permute-start(f32[3,1,8,512]{3,0,2,1:T(4,128)S(1)} %slice.331), channel_id=1, source_target_pairs={{0,8},{8,16},{16,24},{1,9},{9,17},{17,25},{2,10},{10,18},{18,26},{... | collective-permute-start | bytes 147464 | tf_op jit(solution)/shard_map/ppermute | solution.py:12
  86.4 4.4 %collective-permute-start.3 = (f32[3,8,1,512]{3,0,2,1:T(4,128)S(1)}, f32[3,8,1,512]{3,0,2,1:T(4,128)S(1)}, u32[]{:S(2)}, u32[]{:S(2)}) collective-permute-start(f32[3,8,1,512]{3,0,2,1:T(4,128)S(1)} %slice.333), channel_id=1, source_target_pairs={{0,1},{1,2},{2,3},{3,4},{4,5},{5,6},{6,7},{8,9},{9,10},{10,11},{11... | collective-permute-start | bytes 147464 | tf_op jit(solution)/shard_map/ppermute | solution.py:12
  91.0 2.3 %collective-permute-done.3 = f32[3,8,1,512]{3,0,2,1:T(4,128)S(1)} collective-permute-done((f32[3,8,1,512]{3,0,2,1:T(4,128)S(1)}, f32[3,8,1,512]{3,0,2,1:T(4,128)S(1)}, u32[]{:S(2)}, u32[]{:S(2)}) %collective-permute-start.3) | collective-permute-done | bytes 49184 | tf_op jit(solution)/shard_map/ppermute | solution.py:12
  93.3 0.9 fusion.3
  94.1 0.6 multiply_add_fusion.8
  94.8 0.4 pad_maximum_fusion.3
  95.2 0.1 slice_subtract_fusion.5
  95.3 0.3 slice_subtract_fusion.1
  95.6 1.3 collective-permute-start.5
  96.9 0.1 slice_subtract_fusion.6
  97.0 1.5 collective-permute-start.4
  98.5 3.9 %collective-permute-done.5 = f32[3,8,1,512]{3,0,2,1:T(4,128)S(1)} collective-permute-done((f32[3,8,1,512]{3,0,2,1:T(4,128)S(1)}, f32[3,8,1,512]{3,0,2,1:T(4,128)S(1)}, u32[]{:S(2)}, u32[]{:S(2)}) %collective-permute-start.5) | collective-permute-done | bytes 49184 | tf_op jit(solution)/shard_map/ppermute | solution.py:12
  102.4 1.7 %multiply_reduce_fusion.3 = (f32[8,8,512]{2,1,0:T(8,128)S(1)}, f32[3,8,8,512]{3,0,2,1:T(4,128)S(1)}, f32[8,8,512]{2,1,0:T(8,128)S(1)}, f32[3,8,8,512]{3,0,2,1:T(...) fusion(f32[8,8,512]{2,1,0:T(8,128)S(1)} %maximum_divide_fusion.2, ...), kind=kLoop, calls=%fused_computation.43 | loop fusion | flops 1474560 | bytes 4061696 | tf_op jit(solution)/shard_map/reduce_sum | solution.py:84
  104.2 0.7 multiply_subtract_fusion.3
  105.0 2.3 %collective-permute-start.6 = (f32[3,1,8,512]{3,0,2,1:T(4,128)S(1)}, f32[3,1,8,512]{3,0,2,1:T(4,128)S(1)}, u32[]{:S(2)}, u32[]{:S(2)}) collective-permute-start(f32[3,1,8,512]{3,0,2,1:T(4,128)S(1)} %slice.349), channel_id=1, source_target_pairs={{0,8},{8,16},{16,24},{1,9},{9,17},{17,25},{2,10},{10,18},{18,26},{... | collective-permute-start | bytes 147464 | tf_op jit(solution)/shard_map/ppermute | solution.py:12
  107.3 5.0 %collective-permute-start.7 = (f32[3,8,1,512]{3,0,2,1:T(4,128)S(1)}, f32[3,8,1,512]{3,0,2,1:T(4,128)S(1)}, u32[]{:S(2)}, u32[]{:S(2)}) collective-permute-start(f32[3,8,1,512]{3,0,2,1:T(4,128)S(1)} %slice.351), channel_id=1, source_target_pairs={{0,1},{1,2},{2,3},{3,4},{4,5},{5,6},{6,7},{8,9},{9,10},{10,11},{11... | collective-permute-start | bytes 147464 | tf_op jit(solution)/shard_map/ppermute | solution.py:12
  112.3 0.1 slice.350
  112.4 1.7 %collective-permute-done.7 = f32[3,8,1,512]{3,0,2,1:T(4,128)S(1)} collective-permute-done((f32[3,8,1,512]{3,0,2,1:T(4,128)S(1)}, f32[3,8,1,512]{3,0,2,1:T(4,128)S(1)}, u32[]{:S(2)}, u32[]{:S(2)}) %collective-permute-start.7) | collective-permute-done | bytes 49184 | tf_op jit(solution)/shard_map/ppermute | solution.py:12
  114.1 0.8 fusion.7
  115.0 0.6 multiply_add_fusion.5
  115.6 0.4 pad_maximum_fusion.4
  116.0 0.1 slice_subtract_fusion.3
  116.1 0.3 slice_subtract_fusion
  116.5 1.3 collective-permute-start.9
  117.9 1.3 collective-permute-start.8
  119.2 4.1 %collective-permute-done.9 = f32[3,8,1,512]{3,0,2,1:T(4,128)S(1)} collective-permute-done((f32[3,8,1,512]{3,0,2,1:T(4,128)S(1)}, f32[3,8,1,512]{3,0,2,1:T(4,128)S(1)}, u32[]{:S(2)}, u32[]{:S(2)}) %collective-permute-start.9) | collective-permute-done | bytes 49184 | tf_op jit(solution)/shard_map/ppermute | solution.py:12
  123.3 1.4 multiply_reduce_fusion.1
  124.8 0.7 multiply_subtract_fusion
  125.5 1.5 %collective-permute-start.10 = (f32[3,1,8,512]{3,0,2,1:T(4,128)S(1)}, f32[3,1,8,512]{3,0,2,1:T(4,128)S(1)}, u32[]{:S(2)}, u32[]{:S(2)}) collective-permute-start(f32[3,1,8,512]{3,0,2,1:T(4,128)S(1)} %slice.367), channel_id=1, source_target_pairs={{0,8},{8,16},{16,24},{1,9},{9,17},{17,25},{2,10},{10,18},{18,26},{... | collective-permute-start | bytes 147464 | tf_op jit(solution)/shard_map/ppermute | solution.py:12
  127.1 5.2 %collective-permute-start.11 = (f32[3,8,1,512]{3,0,2,1:T(4,128)S(1)}, f32[3,8,1,512]{3,0,2,1:T(4,128)S(1)}, u32[]{:S(2)}, u32[]{:S(2)}) collective-permute-start(f32[3,8,1,512]{3,0,2,1:T(4,128)S(1)} %slice.369), channel_id=1, source_target_pairs={{0,1},{1,2},{2,3},{3,4},{4,5},{5,6},{6,7},{8,9},{9,10},{10,11},{11... | collective-permute-start | bytes 147464 | tf_op jit(solution)/shard_map/ppermute | solution.py:12
  132.5 1.7 %collective-permute-done.11 = f32[3,8,1,512]{3,0,2,1:T(4,128)S(1)} collective-permute-done((f32[3,8,1,512]{3,0,2,1:T(4,128)S(1)}, f32[3,8,1,512]{3,0,2,1:T(4,128)S(1)}, u32[]{:S(2)}, u32[]{:S(2)}) %collective-permute-start.11) | collective-permute-done | bytes 49184 | tf_op jit(solution)/shard_map/ppermute | solution.py:12
  134.2 0.9 fusion.11
  135.0 0.6 multiply_add_fusion.2
  135.7 0.4 pad_maximum_fusion.5
  136.0 0.1 copy.17
  136.2 16.9 %all_to_all.36 = f32[3,8,8,512]{3,2,0,1:T(8,128)S(1)} all-to-all(f32[3,8,8,512]{3,2,0,1:T(8,128)S(1)} %copy.17), channel_id=1, replica_groups=mesh['bin'=4,'slab'=8] {'slab'}, dimensions={1} | all-to-all | bytes 786432 | tf_op jit(solution)/shard_map/all_to_all | solution.py:119
  153.0 0.8 copy.23
  (38 shorter events, 1.2 us)
Async XLA Ops:
  0.0 45.6 %copy-start = (f32[8,3]{0,1:T(4,128)S(1)}, f32[8,3]{0,1:T(4,128)}, u32[]{:S(2)}) copy-start(f32[8,3]{0,1:T(4,128)} %param.5) | copy-start | bytes 292
  41.4 30.5 %all-to-all-start.1 = ((f32[2,32,8,512]{3,2,0,1:T(8,128)}), f32[2,32,8,512]{3,2,0,1:T(8,128)S(1)}, u32[]{:S(2)}, u32[]{:S(2)}) async-start(f32[2,32,8,512]{3,2,0,1:T(8,128)} %copy.14), calls=%async_computation.1 | async-start | bytes 2097152 | tf_op jit(solution)/shard_map/all_to_all | solution.py:94
  76.0 6.4 %collective-permute-start.1 = (f32[3,8,1,512]{3,0,2,1:T(4,128)S(1)}, f32[3,8,1,512]{3,0,2,1:T(4,128)S(1)}, u32[]{:S(2)}, u32[]{:S(2)}) collective-permute-start(f32[3,8,1,512]{3,0,2,1:T(4,128)S(1)} %slice.327), channel_id=1, source_target_pairs={{1,0},{2,1},{3,2},{4,3},{5,4},{6,5},{7,6},{9,8},{10,9},{11,10},{12... | collective-permute-start | bytes 147464 | tf_op jit(solution)/shard_map/ppermute | solution.py:12
  77.4 5.3 %collective-permute-start = (f32[3,1,8,512]{3,0,2,1:T(4,128)S(1)}, f32[3,1,8,512]{3,0,2,1:T(4,128)S(1)}, u32[]{:S(2)}, u32[]{:S(2)}) collective-permute-start(f32[3,1,8,512]{3,0,2,1:T(4,128)S(1)} %slice.323), channel_id=1, source_target_pairs={{8,0},{16,8},{24,16},{9,1},{17,9},{25,17},{10,2},{18,10},{26,18},{... | collective-permute-start | bytes 147464 | tf_op jit(solution)/shard_map/ppermute | solution.py:12
  83.8 7.2 %collective-permute-start.2 = (f32[3,1,8,512]{3,0,2,1:T(4,128)S(1)}, f32[3,1,8,512]{3,0,2,1:T(4,128)S(1)}, u32[]{:S(2)}, u32[]{:S(2)}) collective-permute-start(f32[3,1,8,512]{3,0,2,1:T(4,128)S(1)} %slice.331), channel_id=1, source_target_pairs={{0,8},{8,16},{16,24},{1,9},{9,17},{17,25},{2,10},{10,18},{18,26},{... | collective-permute-start | bytes 147464 | tf_op jit(solution)/shard_map/ppermute | solution.py:12
  86.4 6.9 %collective-permute-start.3 = (f32[3,8,1,512]{3,0,2,1:T(4,128)S(1)}, f32[3,8,1,512]{3,0,2,1:T(4,128)S(1)}, u32[]{:S(2)}, u32[]{:S(2)}) collective-permute-start(f32[3,8,1,512]{3,0,2,1:T(4,128)S(1)} %slice.333), channel_id=1, source_target_pairs={{0,1},{1,2},{2,3},{3,4},{4,5},{5,6},{6,7},{8,9},{9,10},{10,11},{11... | collective-permute-start | bytes 147464 | tf_op jit(solution)/shard_map/ppermute | solution.py:12
  95.6 6.8 %collective-permute-start.5 = (f32[3,8,1,512]{3,0,2,1:T(4,128)S(1)}, f32[3,8,1,512]{3,0,2,1:T(4,128)S(1)}, u32[]{:S(2)}, u32[]{:S(2)}) collective-permute-start(f32[3,8,1,512]{3,0,2,1:T(4,128)S(1)} %slice.345), channel_id=1, source_target_pairs={{1,0},{2,1},{3,2},{4,3},{5,4},{6,5},{7,6},{9,8},{10,9},{11,10},{12... | collective-permute-start | bytes 147464 | tf_op jit(solution)/shard_map/ppermute | solution.py:12
  97.0 5.4 %collective-permute-start.4 = (f32[3,1,8,512]{3,0,2,1:T(4,128)S(1)}, f32[3,1,8,512]{3,0,2,1:T(4,128)S(1)}, u32[]{:S(2)}, u32[]{:S(2)}) collective-permute-start(f32[3,1,8,512]{3,0,2,1:T(4,128)S(1)} %slice.341), channel_id=1, source_target_pairs={{8,0},{16,8},{24,16},{9,1},{17,9},{25,17},{10,2},{18,10},{26,18},{... | collective-permute-start | bytes 147464 | tf_op jit(solution)/shard_map/ppermute | solution.py:12
  105.0 7.5 %collective-permute-start.6 = (f32[3,1,8,512]{3,0,2,1:T(4,128)S(1)}, f32[3,1,8,512]{3,0,2,1:T(4,128)S(1)}, u32[]{:S(2)}, u32[]{:S(2)}) collective-permute-start(f32[3,1,8,512]{3,0,2,1:T(4,128)S(1)} %slice.349), channel_id=1, source_target_pairs={{0,8},{8,16},{16,24},{1,9},{9,17},{17,25},{2,10},{10,18},{18,26},{... | collective-permute-start | bytes 147464 | tf_op jit(solution)/shard_map/ppermute | solution.py:12
  107.3 6.9 %collective-permute-start.7 = (f32[3,8,1,512]{3,0,2,1:T(4,128)S(1)}, f32[3,8,1,512]{3,0,2,1:T(4,128)S(1)}, u32[]{:S(2)}, u32[]{:S(2)}) collective-permute-start(f32[3,8,1,512]{3,0,2,1:T(4,128)S(1)} %slice.351), channel_id=1, source_target_pairs={{0,1},{1,2},{2,3},{3,4},{4,5},{5,6},{6,7},{8,9},{9,10},{10,11},{11... | collective-permute-start | bytes 147464 | tf_op jit(solution)/shard_map/ppermute | solution.py:12
  116.5 6.8 %collective-permute-start.9 = (f32[3,8,1,512]{3,0,2,1:T(4,128)S(1)}, f32[3,8,1,512]{3,0,2,1:T(4,128)S(1)}, u32[]{:S(2)}, u32[]{:S(2)}) collective-permute-start(f32[3,8,1,512]{3,0,2,1:T(4,128)S(1)} %slice.363), channel_id=1, source_target_pairs={{1,0},{2,1},{3,2},{4,3},{5,4},{6,5},{7,6},{9,8},{10,9},{11,10},{12... | collective-permute-start | bytes 147464 | tf_op jit(solution)/shard_map/ppermute | solution.py:12
  117.9 5.4 %collective-permute-start.8 = (f32[3,1,8,512]{3,0,2,1:T(4,128)S(1)}, f32[3,1,8,512]{3,0,2,1:T(4,128)S(1)}, u32[]{:S(2)}, u32[]{:S(2)}) collective-permute-start(f32[3,1,8,512]{3,0,2,1:T(4,128)S(1)} %slice.359), channel_id=1, source_target_pairs={{8,0},{16,8},{24,16},{9,1},{17,9},{25,17},{10,2},{18,10},{26,18},{... | collective-permute-start | bytes 147464 | tf_op jit(solution)/shard_map/ppermute | solution.py:12
  125.5 6.9 %collective-permute-start.10 = (f32[3,1,8,512]{3,0,2,1:T(4,128)S(1)}, f32[3,1,8,512]{3,0,2,1:T(4,128)S(1)}, u32[]{:S(2)}, u32[]{:S(2)}) collective-permute-start(f32[3,1,8,512]{3,0,2,1:T(4,128)S(1)} %slice.367), channel_id=1, source_target_pairs={{0,8},{8,16},{16,24},{1,9},{9,17},{17,25},{2,10},{10,18},{18,26},{... | collective-permute-start | bytes 147464 | tf_op jit(solution)/shard_map/ppermute | solution.py:12
  127.1 7.1 %collective-permute-start.11 = (f32[3,8,1,512]{3,0,2,1:T(4,128)S(1)}, f32[3,8,1,512]{3,0,2,1:T(4,128)S(1)}, u32[]{:S(2)}, u32[]{:S(2)}) collective-permute-start(f32[3,8,1,512]{3,0,2,1:T(4,128)S(1)} %slice.369), channel_id=1, source_target_pairs={{0,1},{1,2},{2,3},{3,4},{4,5},{5,6},{6,7},{8,9},{9,10},{10,11},{11... | collective-permute-start | bytes 147464 | tf_op jit(solution)/shard_map/ppermute | solution.py:12
